TPU v7x, 32 devices: a whole 2x2x4 slice. The times are simulated.
32 devices in a mesh: seq: 8 (over y, x, core), head: 4 (over z).
Axes of the slice: x: 2, y: 2, z: 4, core: 2. Of those that a mesh axis runs over, the one named last changes fastest.
Arguments:
- tokens: float32 [2048, 1024], P('seq'), may hold values from -6 to 6
- doc_start: int32 [2048], P('seq'), may hold values from 0 to 1, as said below
- cotangent: float32 [2048, 1024], P('seq'), may hold values from -6 to 6
- norm_in: float32 [1024], replicated, may hold values from 0.5 to 1.5
- w_in: float32 [1024, 8, 768], P('seq', 'head'), may hold values from -0.1875 to 0.1875
- w_gates: float32 [1024, 2, 8], P('seq', None, 'head'), may hold values from -0.1875 to 0.1875
- conv_w: float32 [4, 8, 512], P(None, 'head'), may hold values from -3 to 3
- decay: float32 [2, 8], P(None, 'head')
- norm_out: float32 [256], replicated, may hold values from 0.5 to 1.5
- w_out: float32 [8, 256, 1024], P('head', None, 'seq'), may hold values from -0.125 to 0.125
- norm_ffn: float32 [1024], replicated, may hold values from 0.5 to 1.5
- w_up: float32 [1024, 2, 2816], P('seq', None, 'head'), may hold values from -0.1875 to 0.1875
- w_down: float32 [2816, 1024], P('head', 'seq'), may hold values from -0.109375 to 0.109375
- moment_norm_in: float32 [1024], replicated, may hold values from -80 to 80
- moment_w_in: float32 [1024, 8, 768], P('seq', 'head'), may hold values from -80 to 80
- moment_w_gates: float32 [1024, 2, 8], P('seq', None, 'head'), may hold values from -80 to 80
- moment_conv_w: float32 [4, 8, 512], P(None, 'head'), may hold values from -80 to 80
- moment_decay: float32 [2, 8], P(None, 'head'), may hold values from -80 to 80
- moment_norm_out: float32 [256], replicated, may hold values from -80 to 80
- moment_w_out: float32 [8, 256, 1024], P('head', None, 'seq'), may hold values from -80 to 80
- moment_norm_ffn: float32 [1024], replicated, may hold values from -80 to 80
- moment_w_up: float32 [1024, 2, 2816], P('seq', None, 'head'), may hold values from -80 to 80
- moment_w_down: float32 [2816, 1024], P('head', 'seq'), may hold values from -80 to 80
Outputs:
- output: float32 [2048, 1024], P('seq')
- grad_tokens: float32 [2048, 1024], P('seq')
- grad_norm_in: float32 [1024], replicated
- grad_w_in: float32 [1024, 8, 768], P('seq', 'head')
- grad_w_gates: float32 [1024, 2, 8], P('seq', None, 'head')
- grad_conv_w: float32 [4, 8, 512], P(None, 'head')
- grad_decay: float32 [2, 8], P(None, 'head')
- grad_norm_out: float32 [256], replicated
- grad_w_out: float32 [8, 256, 1024], P('head', None, 'seq')
- grad_norm_ffn: float32 [1024], replicated
- grad_w_up: float32 [1024, 2, 2816], P('seq', None, 'head')
- grad_w_down: float32 [2816, 1024], P('head', 'seq')
- new_norm_in: float32 [1024], replicated
- new_w_in: float32 [1024, 8, 768], P('seq', 'head')
- new_w_gates: float32 [1024, 2, 8], P('seq', None, 'head')
- new_conv_w: float32 [4, 8, 512], P(None, 'head')
- new_decay: float32 [2, 8], P(None, 'head')
- new_norm_out: float32 [256], replicated
- new_w_out: float32 [8, 256, 1024], P('head', None, 'seq')
- new_norm_ffn: float32 [1024], replicated
- new_w_up: float32 [1024, 2, 2816], P('seq', None, 'head')
- new_w_down: float32 [2816, 1024], P('head', 'seq')
- new_moment_norm_in: float32 [1024], replicated
- new_moment_w_in: float32 [1024, 8, 768], P('seq', 'head')
- new_moment_w_gates: float32 [1024, 2, 8], P('seq', None, 'head')
- new_moment_conv_w: float32 [4, 8, 512], P(None, 'head')
- new_moment_decay: float32 [2, 8], P(None, 'head')
- new_moment_norm_out: float32 [256], replicated
- new_moment_w_out: float32 [8, 256, 1024], P('head', None, 'seq')
- new_moment_norm_ffn: float32 [1024], replicated
- new_moment_w_up: float32 [1024, 2, 2816], P('seq', None, 'head')
- new_moment_w_down: float32 [2816, 1024], P('head', 'seq')
Inputs may be any that keep to these rules, and one draw needn't show every extreme that they name: `doc_start`: exactly two entries are 1: one at a position from 1 to 1023, one from 1024 to 2047.
All inputs are finite; a program needn't handle non-finite values.
Results may differ from a plain program's by a relative error of at most 0.023.
Values may be sent and summed in bfloat16 or wider, within the bound.
A program may use at most 128 MiB of HBM per device.

v0:
```python
import math

import jax
import jax.numpy as jnp
from jax import lax
from jax.sharding import PartitionSpec as P

D = 1024
KEY_SIZE = 128
VALUE_SIZE = 256
CONV = 4
BLOCK_TOKENS = 64
FG = 352
QKVG = 768
CONV_CH = 512


EPSILON = 1e-06
MOMENTUM = 0.95
RATE = 0.05
RATE_SMALL = 0.3
NEWTON_A = 3.4445
NEWTON_B = -4.775
NEWTON_C = 2.0315
NEWTON_STEPS = 5
HIGHEST_LEVEL = lax.Precision.HIGHEST


def shifted_2(block, axis, distance):
    devices = range(lax.axis_size(axis))
    route = [(i - distance, i) for i in devices if i - distance in devices]
    return lax.ppermute(block, axis, route)


def carried_in(value, axis, join, neutral):
    place = lax.axis_index(axis)
    gathered = jax.tree.map(
        lambda a, kind: lax.all_gather(a.astype(kind), axis), value, (jnp.bfloat16, jnp.bfloat16)
    )
    state = jax.tree.map(lambda a, e: jnp.zeros_like(a) + jnp.asarray(e, a.dtype), value, neutral)

    def carried_one(step, state):
        return join(
            state,
            jax.tree.map(
                lambda a, own: lax.dynamic_index_in_dim(a, step, 0, False).astype(own.dtype),
                gathered,
                value,
            ),
        )

    return lax.fori_loop(0, place, carried_one, state)


def entering(value, axis, join, neutral):
    count = lax.axis_size(axis)
    place = lax.axis_index(axis)
    ahead = count - 1 - place
    gathered = jax.tree.map(
        lambda a, kind: lax.all_gather(a.astype(kind), axis),
        value,
        jax.tree.map(lambda a: jnp.bfloat16 if a.dtype == jnp.float32 else a.dtype, value),
    )
    state = jax.tree.map(lambda a, e: jnp.zeros_like(a) + jnp.asarray(e, a.dtype), value, neutral)

    def entering_one(step, state):
        source = count - 1 - step
        return join(
            state,
            jax.tree.map(
                lambda a, own: lax.dynamic_index_in_dim(a, source, 0, False).astype(own.dtype),
                gathered,
                value,
            ),
        )

    return lax.fori_loop(0, ahead, entering_one, state)


def silu(value):
    return value * jax.nn.sigmoid(value)


def rms_unit(value_rows):
    return value_rows * lax.rsqrt(
        jnp.mean(value_rows * value_rows, axis=-1, keepdims=True) + EPSILON
    )


def rms_apply(value_rows, gain):
    return rms_unit(value_rows) * gain


def rms_back(value_rows, gain, upstream):
    scale = lax.rsqrt(jnp.mean(value_rows * value_rows, axis=-1, keepdims=True) + EPSILON)
    unit = value_rows * scale
    inner = upstream * gain
    return scale * (inner - unit * jnp.mean(inner * unit, axis=-1, keepdims=True))


def keep_factors(document_start_mask):
    length = document_start_mask.shape[0]
    alive = 1.0 - document_start_mask
    padded = jnp.concatenate([jnp.ones((CONV - 1,), jnp.float32), alive])
    columns = [jnp.ones((length,), jnp.float32)]
    for tap in range(1, CONV):
        columns.append(columns[-1] * padded[CONV - tap : CONV - tap + length])
    return jnp.stack(columns, 1)


def tail_factors(alive):
    length = alive.shape[0]
    factors = [jnp.ones((), jnp.float32)]
    for back in range(1, CONV - 1):
        factors.insert(0, factors[0] * alive[length - back])
    return jnp.stack(factors)


def convolve(extended, conv_w, keep):
    length = keep.shape[0]
    total_sum = jnp.zeros((length,) + extended.shape[1:], jnp.float32)
    for tap in range(CONV):
        total_sum = (
            total_sum
            + conv_w[tap]
            * extended[CONV - 1 - tap : CONV - 1 - tap + length]
            * keep[:, tap, None, None]
        )
    return total_sum


def apply_activation(mixed_tokens, output_logits, decay):
    active = silu(mixed_tokens)
    query_rows = active[..., :KEY_SIZE]
    key_rows = active[..., KEY_SIZE : 2 * KEY_SIZE]
    value_rows = active[..., 2 * KEY_SIZE :]
    query_rows = (
        query_rows
        * lax.rsqrt(jnp.sum(query_rows * query_rows, axis=-1, keepdims=True) + EPSILON)
        * KEY_SIZE ** (-0.5)
    )
    key_rows = key_rows * lax.rsqrt(jnp.sum(key_rows * key_rows, axis=-1, keepdims=True) + EPSILON)
    write_strength = jax.nn.sigmoid(output_logits[:, 1])
    gate_logarithm = -jnp.exp(decay[0]) * jax.nn.softplus(output_logits[:, 0] + decay[1])
    return (query_rows, key_rows, value_rows, write_strength, gate_logarithm)


def block_list(array):
    return jnp.moveaxis(array.reshape((-1, BLOCK_TOKENS) + array.shape[1:]), 2, 0)


def unblocks(array):
    shifted = jnp.moveaxis(array, 0, 2)
    return shifted.reshape((-1,) + shifted.shape[2:])


def block_recurrence(
    query_rows, key_rows, value_rows, write_strength, gate_logarithm, block_spans, initial_state
):
    size = query_rows.shape[2]
    total_sum = jnp.cumsum(gate_logarithm, axis=-1)
    count = jnp.cumsum(block_spans, axis=-1)
    places = jnp.arange(size)
    lower = places[:, None] >= places[None, :]
    strict = (places[:, None] > places[None, :]).astype(jnp.float32)
    same = (count[:, :, None] == count[:, None, :]) & lower
    spread = total_sum[..., :, None] - total_sum[..., None, :]
    decay_mat = jnp.where(same, jnp.exp(jnp.where(same, spread, 0.0)), 0.0)
    head_part = jnp.exp(total_sum) * (count == 0).astype(jnp.float32)
    tail_part = jnp.exp(total_sum[..., -1:] - total_sum) * (count == count[:, -1:]).astype(
        jnp.float32
    )
    identity = jnp.eye(size, dtype=jnp.float32)
    keys_beta = key_rows * write_strength[..., None]
    negated = (
        -jnp.einsum("bncd,bnmd->bncm", keys_beta, key_rows, precision=HIGHEST_LEVEL)
        * decay_mat
        * strict
    )
    inverse = identity + negated
    power = negated
    for level in range(size.bit_length() - 2):
        power = jnp.einsum("bncm,bnmj->bncj", power, power, precision=HIGHEST_LEVEL)
        inverse = jnp.einsum("bncm,bnmj->bncj", inverse, identity + power, precision=HIGHEST_LEVEL)
    weights = jnp.einsum(
        "bncm,bnmd->bncd", inverse, keys_beta * head_part[..., None], precision=HIGHEST_LEVEL
    )
    targets = jnp.einsum(
        "bncm,bnmw->bncw", inverse, value_rows * write_strength[..., None], precision=HIGHEST_LEVEL
    )
    scores = (
        jnp.einsum("bncd,bnmd->bncm", query_rows, key_rows, precision=HIGHEST_LEVEL) * decay_mat
    )

    def leading(array):
        return jnp.moveaxis(array, 1, 0)

    pieces = (
        leading(query_rows * head_part[..., None]),
        leading(weights),
        leading(targets),
        leading(scores),
        leading(key_rows * tail_part[..., None]),
        leading(head_part[..., -1]),
    )

    def advance(state, piece):
        queries, weight, target, score, keyed, last = piece
        fresh_value = target - jnp.einsum("bcd,bdw->bcw", weight, state, precision=HIGHEST_LEVEL)
        result = jnp.einsum("bcd,bdw->bcw", queries, state, precision=HIGHEST_LEVEL) + jnp.einsum(
            "bcm,bmw->bcw", score, fresh_value, precision=HIGHEST_LEVEL
        )
        state = last[:, None, None] * state + jnp.einsum(
            "bcd,bcw->bdw", keyed, fresh_value, precision=HIGHEST_LEVEL
        )
        return (state, result)

    final_state, block_results = lax.scan(advance, initial_state, pieces)
    return (jnp.moveaxis(block_results, 0, 1), final_state)


def gated_norm(attended_output, gate_part, norm_out):
    return rms_apply(attended_output, norm_out) * silu(gate_part)


def compose(earlier, later):
    return (
        jnp.einsum("hij,hjk->hik", later[0], earlier[0], precision=HIGHEST_LEVEL),
        jnp.einsum("hij,hjv->hiv", later[0], earlier[1], precision=HIGHEST_LEVEL) + later[1],
    )


def head_total(partial_sum):
    return lax.psum(partial_sum.astype(jnp.bfloat16), "head").astype(jnp.float32)


def newton_turn(current, gram_sum):
    gram = gram_sum.astype(jnp.bfloat16)
    poly = (
        NEWTON_B * gram.astype(jnp.float32)
        + NEWTON_C
        * jnp.einsum("...ij,...jk->...ik", gram, gram, preferred_element_type=jnp.float32)
    ).astype(jnp.bfloat16)
    return (
        NEWTON_A * current.astype(jnp.float32)
        + jnp.einsum("...ri,...ij->...rj", current, poly, preferred_element_type=jnp.float32)
    ).astype(jnp.bfloat16)


def newton_schulz(batch):
    wide = batch.astype(jnp.float32)
    total_sum = jnp.sum(wide * wide, axis=(1, 2), keepdims=True)
    current = (wide / (jnp.sqrt(total_sum) + 1e-07)).astype(jnp.bfloat16)
    for turn in range(NEWTON_STEPS):
        current = newton_turn(
            current,
            jnp.einsum("bri,brj->bij", current, current, preferred_element_type=jnp.float32),
        )
    return current


def per_device(
    tokens,
    doc_start,
    cotangent,
    norm_in,
    w_in,
    w_gates,
    conv_w,
    decay,
    norm_out,
    w_out,
    norm_ffn,
    w_up,
    w_down,
    moment_norm_in,
    moment_w_in,
    moment_w_gates,
    moment_conv_w,
    moment_decay,
    moment_norm_out,
    moment_w_out,
    moment_norm_ffn,
    moment_w_up,
    moment_w_down,
):
    length = tokens.shape[0]
    head_count = w_in.shape[1]
    hidden = w_up.shape[2]
    owners = lax.axis_size("seq")
    full_in, full_gates, full_out, full_up, full_down = (
        lax.all_gather(w_in.astype(jnp.bfloat16), "seq", axis=0, tiled=True),
        lax.all_gather(w_gates.astype(jnp.bfloat16), "seq", axis=0, tiled=True),
        lax.all_gather(w_out.astype(jnp.bfloat16), "seq", axis=2, tiled=True),
        lax.all_gather(w_up.astype(jnp.bfloat16), "seq", axis=0, tiled=True),
        lax.all_gather(w_down.astype(jnp.bfloat16), "seq", axis=1, tiled=True),
    )
    document_start_mask = doc_start.astype(jnp.float32)
    alive = 1.0 - document_start_mask
    unit_in = rms_unit(tokens)
    normed_in = (unit_in * norm_in).astype(jnp.bfloat16)
    proj = lax.optimization_barrier(
        jnp.einsum("td,dhc->thc", normed_in, full_in, preferred_element_type=jnp.float32).astype(
            jnp.bfloat16
        )
    )
    output_logits = jnp.einsum(
        "td,dgh->tgh", normed_in, full_gates, preferred_element_type=jnp.float32
    )
    conv_in = proj[..., :CONV_CH]
    gate_part = proj[..., CONV_CH:].astype(jnp.float32)
    edge_scale = tail_factors(alive)
    edge = (conv_in[length - CONV + 1 :].astype(jnp.float32) * edge_scale[:, None, None]).astype(
        jnp.bfloat16
    )
    before = shifted_2(edge, "seq", 1)
    extended = jnp.concatenate([before, conv_in]).astype(jnp.float32)
    keep = keep_factors(document_start_mask)
    block_spans = document_start_mask.reshape(-1, BLOCK_TOKENS)
    identity = jnp.broadcast_to(
        jnp.eye(KEY_SIZE, dtype=jnp.float32), (head_count, KEY_SIZE, KEY_SIZE)
    )
    empty = jnp.zeros((head_count, KEY_SIZE, VALUE_SIZE), jnp.float32)

    def local_pass(extended, conv_w, output_logits, decay):
        mixed_tokens = convolve(extended, conv_w, keep)
        query_rows, key_rows, value_rows, write_strength, gate_logarithm = apply_activation(
            mixed_tokens, output_logits, decay
        )
        stacked = jnp.concatenate(
            [jnp.zeros(value_rows.shape[:-1] + (KEY_SIZE,), jnp.float32), value_rows], -1
        )
        block_results, final_state = block_recurrence(
            block_list(query_rows),
            block_list(key_rows),
            block_list(stacked),
            block_list(write_strength),
            block_list(gate_logarithm),
            block_spans,
            jnp.concatenate([identity, empty], -1),
        )
        block_results = unblocks(block_results)
        return (
            block_results[..., :KEY_SIZE],
            block_results[..., KEY_SIZE:],
            final_state[..., :KEY_SIZE],
            final_state[..., KEY_SIZE:],
        )

    def local_core(extended, conv_w, output_logits, decay, incoming_state):
        carried_state, fresh_value, transfer, offset = local_pass(
            extended, conv_w, output_logits, decay
        )
        attended_output = fresh_value + jnp.einsum(
            "usj,sjo->uso", carried_state, incoming_state, precision=HIGHEST_LEVEL
        )
        return (
            attended_output,
            jnp.einsum("hij,hjv->hiv", transfer, incoming_state, precision=HIGHEST_LEVEL) + offset,
        )

    carried_state, fresh_value, transfer, offset = local_pass(
        extended, conv_w, output_logits, decay
    )
    prefix = carried_in((transfer, offset), "seq", compose, (identity, empty))
    incoming_state = prefix[1]
    attended_output = fresh_value + jnp.einsum(
        "usj,sjo->uso", carried_state, incoming_state, precision=HIGHEST_LEVEL
    )
    gated = gated_norm(attended_output, gate_part, norm_out)
    gated_b = gated.astype(jnp.bfloat16)
    residual = tokens + head_total(
        jnp.einsum("thv,hvd->td", gated_b, full_out, preferred_element_type=jnp.float32)
    )
    unit_ffn = rms_unit(residual)
    normed_ffn = (unit_ffn * norm_ffn).astype(jnp.bfloat16)
    ffn_pre = jnp.einsum("td,dgf->tgf", normed_ffn, full_up, preferred_element_type=jnp.float32)
    gate_pre = ffn_pre[:, 0]
    lift = ffn_pre[:, 1]
    active = (silu(gate_pre) * lift).astype(jnp.bfloat16)
    output = residual + head_total(jnp.dot(active, full_down, preferred_element_type=jnp.float32))
    cot_b = cotangent.astype(jnp.bfloat16)
    grad_down_part = jnp.einsum("tf,td->fd", active, cot_b, preferred_element_type=jnp.float32)
    d_active = jnp.einsum("td,fd->tf", cot_b, full_down, preferred_element_type=jnp.float32)
    sigma = jax.nn.sigmoid(gate_pre)
    d_gate_pre = d_active * lift * sigma * (1.0 + gate_pre * (1.0 - sigma))
    d_lift = d_active * gate_pre * sigma
    d_ffn_pre = jnp.stack([d_gate_pre, d_lift], 1).astype(jnp.bfloat16)
    grad_up_part = jnp.einsum(
        "td,tgf->dgf", normed_ffn, d_ffn_pre, preferred_element_type=jnp.float32
    )
    d_ffn_part = jnp.einsum("tgf,dgf->td", d_ffn_pre, full_up, preferred_element_type=jnp.float32)
    gain_ffn_part = jnp.sum(d_ffn_part * unit_ffn, 0)
    d_residual = cotangent + rms_back(residual, norm_ffn, head_total(d_ffn_part))
    res_b = d_residual.astype(jnp.bfloat16)
    grad_out_part = jnp.einsum("thv,td->hvd", gated_b, res_b, preferred_element_type=jnp.float32)
    d_gated = jnp.einsum("td,hvd->thv", res_b, full_out, preferred_element_type=jnp.float32)
    unused_gated, norm_pull = jax.vjp(gated_norm, attended_output, gate_part, norm_out)
    attended_gradient, d_gate_part, gain_out_part = norm_pull(d_gated)
    local_gradient = jnp.einsum(
        "smq,smw->mqw", carried_state, attended_gradient, precision=HIGHEST_LEVEL
    )
    suffix = entering(
        (jnp.swapaxes(transfer, 1, 2), local_gradient), "seq", compose, (identity, empty)
    )
    unused_core, core_pull = jax.vjp(
        local_core, extended, conv_w, output_logits, decay, incoming_state
    )
    d_extended, grad_conv_part, d_logits, grad_decay_part, unused_state = core_pull(
        (attended_gradient, suffix[1])
    )
    returned_edge = shifted_2(d_extended[: CONV - 1], "seq", -1)
    inner = d_extended[CONV - 1 :]
    d_conv_in = jnp.concatenate(
        [
            inner[: length - CONV + 1],
            inner[length - CONV + 1 :] + returned_edge * edge_scale[:, None, None],
        ]
    )
    d_proj = jnp.concatenate([d_conv_in, d_gate_part], -1).astype(jnp.bfloat16)
    d_logits_b = d_logits.astype(jnp.bfloat16)
    grad_in_part = jnp.einsum("td,thc->dhc", normed_in, d_proj, preferred_element_type=jnp.float32)
    grad_gates_part = jnp.einsum(
        "td,tgh->dgh", normed_in, d_logits_b, preferred_element_type=jnp.float32
    )
    d_in_part = jnp.einsum(
        "thc,dhc->td", d_proj, full_in, preferred_element_type=jnp.float32
    ) + jnp.einsum("tgh,dgh->td", d_logits_b, full_gates, preferred_element_type=jnp.float32)
    gain_in_part = jnp.sum(d_in_part * unit_in, 0)
    grad_tokens = d_residual + rms_back(tokens, norm_in, head_total(d_in_part))
    grad_w_in, grad_w_gates, grad_w_out, grad_w_up, grad_w_down = (
        lax.psum_scatter(
            grad_in_part.astype(jnp.bfloat16), "seq", scatter_dimension=0, tiled=True
        ).astype(jnp.float32),
        lax.psum_scatter(
            grad_gates_part.astype(jnp.bfloat16), "seq", scatter_dimension=0, tiled=True
        ).astype(jnp.float32),
        lax.psum_scatter(
            grad_out_part.astype(jnp.bfloat16), "seq", scatter_dimension=2, tiled=True
        ).astype(jnp.float32),
        lax.psum_scatter(
            grad_up_part.astype(jnp.bfloat16), "seq", scatter_dimension=0, tiled=True
        ).astype(jnp.float32),
        lax.psum_scatter(
            grad_down_part.astype(jnp.bfloat16), "seq", scatter_dimension=1, tiled=True
        ).astype(jnp.float32),
    )
    grad_conv_w, grad_decay = lax.psum((grad_conv_part, grad_decay_part), "seq")
    grad_norm_in, grad_norm_out, grad_norm_ffn = lax.psum(
        (gain_in_part, gain_out_part, gain_ffn_part), ("seq", "head")
    )
    small_scale = RATE_SMALL / math.sqrt(length * owners)

    def small_update(weight, moment, grad):
        fresh_moment = MOMENTUM * moment + grad
        return (weight - small_scale * (grad + MOMENTUM * fresh_moment), fresh_moment)

    new_norm_in, new_moment_norm_in = small_update(norm_in, moment_norm_in, grad_norm_in)
    new_w_gates, new_moment_w_gates = small_update(w_gates, moment_w_gates, grad_w_gates)
    new_conv_w, new_moment_conv_w = small_update(conv_w, moment_conv_w, grad_conv_w)
    new_decay, new_moment_decay = small_update(decay, moment_decay, grad_decay)
    new_norm_out, new_moment_norm_out = small_update(norm_out, moment_norm_out, grad_norm_out)
    new_norm_ffn, new_moment_norm_ffn = small_update(norm_ffn, moment_norm_ffn, grad_norm_ffn)
    new_moment_w_in = MOMENTUM * moment_w_in + grad_w_in
    look_in = grad_w_in + MOMENTUM * new_moment_w_in
    new_moment_w_out = MOMENTUM * moment_w_out + grad_w_out
    look_out = grad_w_out + MOMENTUM * new_moment_w_out
    new_moment_w_up = MOMENTUM * moment_w_up + grad_w_up
    look_up = grad_w_up + MOMENTUM * new_moment_w_up
    new_moment_w_down = MOMENTUM * moment_w_down + grad_w_down
    look_down = grad_w_down + MOMENTUM * new_moment_w_down
    bounds = ((0, KEY_SIZE), (KEY_SIZE, 2 * KEY_SIZE), (2 * KEY_SIZE, CONV_CH), (CONV_CH, QKVG))
    pieces = []
    widths = []
    for head in range(head_count):
        for lower_col, upper_col in bounds:
            pieces.append(look_in[:, head, lower_col:upper_col])
            widths.append(upper_col - lower_col)
        pieces.append(look_out[head].T)
        widths.append(VALUE_SIZE)
    groups = hidden // FG
    for group in range(groups):
        pieces.append(look_up[:, 0, group * FG : (group + 1) * FG])
        pieces.append(look_up[:, 1, group * FG : (group + 1) * FG])
        pieces.append(look_down[group * FG : (group + 1) * FG].T)
        widths.extend([FG, FG, FG])
    rounded_pieces = [piece.astype(jnp.bfloat16) for piece in pieces]
    count = len(rounded_pieces)
    rows = rounded_pieces[0].shape[0]
    widest = max(widths)
    per_owner = -(-count // owners)
    padded = [jnp.pad(piece, ((0, 0), (0, widest - piece.shape[1]))) for piece in rounded_pieces]
    padded = padded + [jnp.zeros((rows, widest), jnp.bfloat16)] * (owners * per_owner - count)
    outgoing = jnp.stack(padded).reshape(owners, per_owner, rows, widest)
    finished = newton_schulz(
        lax.all_to_all(outgoing, "seq", split_axis=0, concat_axis=2, tiled=True)[0]
    )[None]
    returned = lax.all_to_all(finished, "seq", split_axis=2, concat_axis=0, tiled=True)
    flat = returned.reshape(owners * per_owner, rows, widest)
    orthos = [flat[index, :, : widths[index]] for index in range(count)]
    updates = [
        orthos[index].astype(jnp.float32) * (RATE * 0.2 * math.sqrt(max(D, widths[index])))
        for index in range(count)
    ]
    cursor = 0
    in_heads = []
    out_heads = []
    for head in range(head_count):
        in_heads.append(jnp.concatenate(updates[cursor : cursor + 4], -1))
        out_heads.append(updates[cursor + 4].T)
        cursor += 5
    gate_cols = []
    lift_cols = []
    down_rows = []
    for group in range(groups):
        gate_cols.append(updates[cursor])
        lift_cols.append(updates[cursor + 1])
        down_rows.append(updates[cursor + 2].T)
        cursor += 3
    new_w_in = w_in - jnp.stack(in_heads, 1)
    new_w_out = w_out - jnp.stack(out_heads, 0)
    new_w_up = w_up - jnp.stack([jnp.concatenate(gate_cols, -1), jnp.concatenate(lift_cols, -1)], 1)
    new_w_down = w_down - jnp.concatenate(down_rows, 0)
    return (
        output,
        grad_tokens,
        grad_norm_in,
        grad_w_in,
        grad_w_gates,
        grad_conv_w,
        grad_decay,
        grad_norm_out,
        grad_w_out,
        grad_norm_ffn,
        grad_w_up,
        grad_w_down,
        new_norm_in,
        new_w_in,
        new_w_gates,
        new_conv_w,
        new_decay,
        new_norm_out,
        new_w_out,
        new_norm_ffn,
        new_w_up,
        new_w_down,
        new_moment_norm_in,
        new_moment_w_in,
        new_moment_w_gates,
        new_moment_conv_w,
        new_moment_decay,
        new_moment_norm_out,
        new_moment_w_out,
        new_moment_norm_ffn,
        new_moment_w_up,
        new_moment_w_down,
    )


def solution(mesh):
    return jax.shard_map(
        per_device,
        mesh=mesh,
        in_specs=(
            P("seq", None),
            P("seq"),
            P("seq", None),
            P(),
            P("seq", "head", None),
            P("seq", None, "head"),
            P(None, "head", None),
            P(None, "head"),
            P(),
            P("head", None, "seq"),
            P(),
            P("seq", None, "head"),
            P("head", "seq"),
            P(),
            P("seq", "head", None),
            P("seq", None, "head"),
            P(None, "head", None),
            P(None, "head"),
            P(),
            P("head", None, "seq"),
            P(),
            P("seq", None, "head"),
            P("head", "seq"),
        ),
        out_specs=(
            P("seq", None),
            P("seq", None),
            P(),
            P("seq", "head", None),
            P("seq", None, "head"),
            P(None, "head", None),
            P(None, "head"),
            P(),
            P("head", None, "seq"),
            P(),
            P("seq", None, "head"),
            P("head", "seq"),
            P(),
            P("seq", "head", None),
            P("seq", None, "head"),
            P(None, "head", None),
            P(None, "head"),
            P(),
            P("head", None, "seq"),
            P(),
            P("seq", None, "head"),
            P("head", "seq"),
            P(),
            P("seq", "head", None),
            P("seq", None, "head"),
            P(None, "head", None),
            P(None, "head"),
            P(),
            P("head", None, "seq"),
            P(),
            P("seq", None, "head"),
            P("head", "seq"),
        ),
        check_vma=False,
    )
```

profile of v0, /device:TPU:0, one launch (start us, length us, event | category | flops | bytes accessed | tf_op | source)
XLA Modules:
  0.0 740.6 jit_solution(12315960248807623033)
XLA Ops:
  9.4 10.3 %all_gather.39 = bf16[1024,2,2]{0,2,1:T(2,128)(2,1)S(1)} all-gather(bf16[128,2,2]{0,2,1:T(2,128)(2,1)S(1)} %convert_element_type.460), channel_id=1, replica_groups=mesh['seq'=8,'head'=4] {'seq'}, dimensions={0}, use_global_device_ids=true | all-gather | bytes 9216 | tf_op jit(solution)/shard_map/all_gather | solution.py:293
  25.3 20.2 %all-gather.11.cloned.1.call-done = bf16[1024,2,768]{2,0,1:T(8,128)(2,1)} async-done(((bf16[128,2,768]{2,0,1:T(8,128)(2,1)}), bf16[1024,2,768]{2,0,1:T(8,128)(2,1)}) %all-gather.11.cloned.1.call-update) | async-done | bytes 3145744 | tf_op jit(solution)/shard_map/all_gather | solution.py:292
  66.1 16.6 %while.80 = (s32[]{:T(128)}, f32[2,128,384]{2,1,0:T(8,128)S(1)}, f32[4,2,64,384]{3,2,1,0:T(8,128)}, f32[4,2]{1,0:T(4,128)S(1)}, f32[4,2,64,128]{3,2,1,0:T(8,128)...) while((s32[]{:T(128)}, f32[2,128,384]{2,1,0:T(8,128)S(1)}, ...), condition=%wide.region_6.7_spmd, body=%wide.region_5.6_spmd.sunk | while | flops 264536064 | bytes 3213961 | solution.py:218
  86.3 13.0 %all-gather = bf16[16,128,128]{2,1,0:T(8,128)(2,1)S(1)} all-gather(bf16[2,128,128]{2,1,0:T(8,128)(2,1)S(1)} %slice.486), channel_id=2, replica_groups=mesh['seq'=8,'head'=4] {'seq'}, dimensions={0}, use_global_device_ids=true | all-gather | bytes 589824 | tf_op jit(solution)/shard_map/all_gather | solution.py:38
  99.3 10.8 %all-gather.19.cloned.1.call-done = bf16[16,128,256]{2,1,0:T(8,128)(2,1)} async-done(((bf16[2,128,256]{2,1,0:T(8,128)(2,1)}), bf16[16,128,256]{2,1,0:T(8,128)(2,1)}) %all-gather.19.cloned.1.call-update) | async-done | bytes 1048592 | tf_op jit(solution)/shard_map/all_gather | solution.py:38
  112.4 23.6 %all-gather.13.cloned.1.call-done = bf16[2,256,1024]{2,1,0:T(8,128)(2,1)} async-done(((bf16[2,256,128]{2,1,0:T(8,128)(2,1)}), bf16[2,256,1024]{2,1,0:T(8,128)(2,1)}) %all-gather.13.cloned.1.call-update) | async-done | bytes 1048592 | tf_op jit(solution)/shard_map/all_gather | solution.py:294
  140.5 37.0 %all-reduce.41.cloned.1.call-done = bf16[256,1024]{1,0:T(8,128)(2,1)} async-done(((bf16[256,1024]{1,0:T(8,128)(2,1)}), bf16[256,1024]{1,0:T(8,128)(2,1)}) %all-reduce.41.cloned.1.call-update) | async-done | bytes 524304 | tf_op jit(solution)/shard_map/psum | solution.py:234
  179.1 32.1 %all-gather.15.cloned.1.call-done = bf16[1024,2,704]{0,2,1:T(8,128)(2,1)} async-done(((bf16[128,2,704]{0,2,1:T(8,128)(2,1)}), bf16[1024,2,704]{0,2,1:T(8,128)(2,1)}) %all-gather.15.cloned.1.call-update) | async-done | bytes 2883600 | tf_op jit(solution)/shard_map/all_gather | solution.py:295
  215.3 23.5 %all-gather.17.cloned.1.call-done = bf16[704,1024]{1,0:T(8,128)(2,1)} async-done(((bf16[704,128]{1,0:T(8,128)(2,1)}), bf16[704,1024]{1,0:T(8,128)(2,1)}) %all-gather.17.cloned.1.call-update) | async-done | bytes 1441808 | tf_op jit(solution)/shard_map/all_gather | solution.py:296
  244.8 38.7 %all-reduce.43.cloned.1.call-done = bf16[256,1024]{1,0:T(8,128)(2,1)} async-done(((bf16[256,1024]{1,0:T(8,128)(2,1)}), bf16[256,1024]{1,0:T(8,128)(2,1)}) %all-reduce.43.cloned.1.call-update) | async-done | bytes 524304 | tf_op jit(solution)/shard_map/psum | solution.py:234
  309.4 19.0 %while.83 = (s32[]{:T(128)}, f32[2,128,384]{2,1,0:T(8,128)S(1)}, f32[4,2,128,384]{3,2,1,0:T(8,128)}, f32[4,2,64,384]{3,2,1,0:T(8,128)}, f32[4,2,1,1]{1,3,2,0:T(1...) while((s32[]{:T(128)}, f32[2,128,384]{2,1,0:T(8,128)S(1)}, ...), condition=%wide.region_19.20_spmd, body=%wide.region_18.19_spmd.sunk | while | flops 151240704 | bytes 2885433 | solution.py:218
  328.6 10.8 %all-gather.2 = bf16[16,128,128]{2,1,0:T(8,128)(2,1)} all-gather(bf16[2,128,128]{2,1,0:T(8,128)(2,1)S(1)} %copy.360), channel_id=4, replica_groups=mesh['seq'=8,'head'=4] {'seq'}, dimensions={0}, use_global_device_ids=true | all-gather | bytes 589824 | tf_op jit(solution)/shard_map/all_gather | solution.py:60
  350.5 9.2 %while.82 = (s32[]{:T(128)}, f32[2,128,256]{2,1,0:T(8,128)S(1)}, s32[]{:T(128)}, bf16[8,2,128,128]{3,2,1,0:T(8,128)(2,1)}, bf16[8,2,128,256]{3,2,1,0:T(8,128)(2,...) while((s32[]{:T(128)}, f32[2,128,256]{2,1,0:T(8,128)S(1)}, s32[]{:T(128)}, ...), condition=%wide.region_17.18_spmd, body=%wide.region_16.17_spmd.sunk | while | flops 100794376 | bytes 1246355 | solution.py:77
  363.8 63.5 %while.84 = (s32[]{:T(128)}, f32[2,128,384]{2,1,0:T(8,128)S(1)}, f32[4,2,64,128]{3,2,1,0:T(8,128)}, f32[4,2,64,128]{3,2,1,0:T(8,128)}, f32[4,2,64,384]{3,2,1,0:T...) while((s32[]{:T(128)}, f32[2,128,384]{2,1,0:T(8,128)S(1)}, ...), condition=%wide.region_22.23_spmd, body=%wide.region_20.22_spmd.sunk | while | flops 529121280 | bytes 16261489 | solution.py:218
  484.9 20.3 %reduce-scatter.16.cloned.1.call-done = bf16[128,1536]{1,0:T(8,128)(2,1)} async-done(((bf16[1024,1536]{1,0:T(8,128)(2,1)}), bf16[128,1536]{1,0:T(8,128)(2,1)}) %reduce-scatter.16.cloned.1.call-update) | async-done | bytes 393232
  514.2 37.0 %all-reduce.35 = (f32[4,2,512]{2,1,0:T(2,128)S(1)}, f32[2,2]{1,0:T(2,128)S(1)}) all-reduce(f32[4,2,512]{2,1,0:T(2,128)S(1)} %pad_add_fusion.4, f32[2,2]{1,0:T(2,128)S(1)} %pad_add_fusion.5), channel_id=1, replica_groups=mesh['seq'=8,'head'=4] {'seq'}, use_global_device_ids=true, to_apply=%region_44.45 | all-reduce | flops 4100 | bytes 32800 | tf_op jit(solution)/shard_map/psum | solution.py:448
  553.9 44.3 %all-reduce.45.cloned.1.call-done = (bf16[256,1024]{1,0:T(8,128)(2,1)}, bf16[256,1024]{1,0:T(8,128)(2,1)}) async-done(((bf16[256,1024]{1,0:T(8,128)(2,1)}, bf16[256,1024]{1,0:T(8,128)(2,1)}), (bf16[256,1024]{1,0:T(8,128)(2,1)}, bf16[256,1024]{1,0:T(8,128)(2,1)})) %all-reduce.45.cloned.1.call-update) | async-done | bytes 1048592 | tf_op jit(solution)/shard_map/psum | solution.py:234
  599.9 40.1 %all-reduce.34 = (f32[1024]{0:T(1024)S(1)}, f32[256]{0:T(256)S(1)}, f32[1024]{0:T(1024)S(1)}) all-reduce(f32[1024]{0:T(1024)S(1)} %get-tuple-element.925, f32[256]{0:T(256)S(1)} %copy-done.160, f32[1024]{0:T(1024)S(1)} %copy-done.126), channel_id=1, replica_groups=mesh['seq'=8,'head'=4] {'seq','head'}, use_global_device_ids=true, to_apply=%region_37.38 | all-reduce | flops 2304 | bytes 18432 | tf_op jit(solution)/shard_map/psum | solution.py:449
  664.9 4.7 add_convert_fusion.3
  673.2 4.7 add_convert_fusion.2
  681.4 4.7 add_convert_fusion.1
  689.6 4.7 fusion.71
  694.3 5.0 copy.409
  709.8 15.0 %all-to-all-done.1 = bf16[1,2,1024,352]{3,1,0,2:T(2,128)(2,1)} async-done(((bf16[1,2,1024,352]{3,1,0,2:T(2,128)(2,1)}), bf16[1,2,1024,352]{3,1,0,2:T(2,128)(2,1)}, u32[]{:S(2)}, u32[]{:S(2)}) %all-to-all-start.1) | async-done | bytes 1441824 | tf_op jit(solution)/shard_map/all_to_all | solution.py:498
  (734 shorter events, 321.4 us)
Async XLA Ops:
  7.2 38.2 %all-gather.11.cloned.1.call-start = ((), (), s32[]{:S(2)}) async-start(), calls=%async_computation.7 | async-start | bytes 3538944 | tf_op jit(solution)/shard_map/all_gather | solution.py:292
  9.3 100.8 %all-gather.19.cloned.1.call-start = ((), (), s32[]{:S(2)}) async-start(), calls=%async_computation.13 | async-start | bytes 1179648 | tf_op jit(solution)/shard_map/all_gather | solution.py:38
  48.5 3.0 collective-permute-start
  83.4 52.7 %all-gather.13.cloned.1.call-start = ((), (), s32[]{:S(2)}) async-start(), calls=%async_computation.8 | async-start | bytes 1179648 | tf_op jit(solution)/shard_map/all_gather | solution.py:294
  84.2 93.4 %all-reduce.41.cloned.1.call-start = ((), (), s32[]{:S(2)}) async-start(), calls=%async_computation.9 | async-start | bytes 1048576 | tf_op jit(solution)/shard_map/psum | solution.py:234
  138.8 72.5 %all-gather.15.cloned.1.call-start = ((), (), s32[]{:S(2)}) async-start(), calls=%async_computation.10 | async-start | bytes 3244032 | tf_op jit(solution)/shard_map/all_gather | solution.py:295
  139.6 99.2 %all-gather.17.cloned.1.call-start = ((), (), s32[]{:S(2)}) async-start(), calls=%async_computation.11 | async-start | bytes 1622016 | tf_op jit(solution)/shard_map/all_gather | solution.py:296
  140.4 143.0 %all-reduce.43.cloned.1.call-start = ((), (), s32[]{:S(2)}) async-start(), calls=%async_computation.12 | async-start | bytes 1048576 | tf_op jit(solution)/shard_map/psum | solution.py:234
  179.1 106.8 %copy-start.116 = (f32[256]{0:T(256)}, f32[256]{0:T(256)S(1)}, u32[]{:S(2)}) copy-start(f32[256]{0:T(256)S(1)} %add_rsqrt_fusion.2) | copy-start | bytes 3076
  244.7 105.7 %all-gather.21.cloned.1.call-start = ((), (), s32[]{:S(2)}) async-start(), calls=%async_computation.14 | async-start | bytes 1179648 | tf_op jit(solution)/shard_map/all_gather | solution.py:60
  293.0 174.7 %reduce-scatter.20.cloned.1.call-start = ((), (), s32[]{:S(2)}) async-start(), calls=%async_computation.17 | async-start | bytes 1179648
  302.1 169.3 %reduce-scatter.24.cloned.1.call-start = ((), (), s32[]{:S(2)}) async-start(), calls=%async_computation.19 | async-start | bytes 1769472
  308.4 174.0 %reduce-scatter.22.cloned.1.call-start = ((), (), s32[]{:S(2)}) async-start(), calls=%async_computation.18 | async-start | bytes 3244032
  347.8 157.4 %reduce-scatter.16.cloned.1.call-start = ((), (), s32[]{:S(2)}) async-start(), calls=%async_computation.15 | async-start | bytes 3538944
  454.2 3.1 collective-permute-start.1
  460.4 92.0 %reduce-scatter.18.cloned.1.call-start = ((), (), s32[]{:S(2)}) async-start(), calls=%async_computation.16 | async-start | bytes 294912
  478.0 120.2 %all-reduce.45.cloned.1.call-start = ((), (), s32[]{:S(2)}) async-start(), calls=%async_computation.20 | async-start | bytes 2097152 | tf_op jit(solution)/shard_map/psum | solution.py:234
  509.7 88.5 %copy-start.7 = (f32[256,1024]{1,0:T(8,128)S(1)}, f32[256,1024]{1,0:T(8,128)}, u32[]{:S(2)}) copy-start(f32[256,1024]{1,0:T(8,128)} %param.33) | copy-start | bytes 3145732
  509.7 130.9 %all-to-all-start = ((bf16[8,2,128,352]{2,3,1,0:T(8,128)(2,1)}), bf16[8,2,128,352]{2,3,1,0:T(8,128)(2,1)}, u32[]{:S(2)}, u32[]{:S(2)}) async-start(bf16[8,2,128,352]{2,3,1,0:T(8,128)(2,1)} %bitcast.749), calls=%async_computation | async-start | bytes 2883584 | tf_op jit(solution)/shard_map/all_to_all | solution.py:496
  514.2 125.8 %copy-start.147 = (f32[256]{0:T(256)S(1)}, f32[256]{0:T(256)}, u32[]{:S(2)}) copy-start(f32[256]{0:T(256)} %param.41) | copy-start | bytes 3076
  514.2 125.8 %copy-start.159 = (f32[256]{0:T(256)S(1)}, f32[256]{0:T(256)}, u32[]{:S(2)}) copy-start(f32[256]{0:T(256)} %param.51) | copy-start | bytes 3076
  551.2 91.0 %copy-start.130 = (f32[4,2,512]{2,1,0:T(2,128)}, f32[4,2,512]{2,1,0:T(2,128)S(1)}, u32[]{:S(2)}) copy-start(f32[4,2,512]{2,1,0:T(2,128)S(1)} %get-tuple-element.1029) | copy-start | bytes 49156
  551.2 91.0 %copy-start.161 = (f32[2,2]{1,0:T(2,128)}, f32[2,2]{1,0:T(2,128)S(1)}, u32[]{:S(2)}) copy-start(f32[2,2]{1,0:T(2,128)S(1)} %get-tuple-element.1030) | copy-start | bytes 52
  699.3 25.5 %all-to-all-start.1 = ((bf16[1,2,1024,352]{3,1,0,2:T(2,128)(2,1)}), bf16[1,2,1024,352]{3,1,0,2:T(2,128)(2,1)}, u32[]{:S(2)}, u32[]{:S(2)}) async-start(bf16[1,2,1024,352]{3,1,0,2:T(2,128)(2,1)} %copy.409), calls=%async_computation.1 | async-start | bytes 3145728 | tf_op jit(solution)/shard_map/all_to_all | solution.py:498
  (170 other events, 1699.7 us)
Sparse Core Ops, SparseCore 0:
  10.5 34.8 all-gather.10
  83.5 26.5 all-gather.18
  112.6 23.4 all-gather.12
  138.9 38.6 all-reduce.40
  179.8 31.3 all-gather.14
  213.6 25.1 all-gather.16
  244.8 38.6 all-reduce.42
  293.1 23.1 all-gather.20
  320.0 35.9 reduce-scatter.19
  359.2 38.3 reduce-scatter.23
  401.0 44.7 reduce-scatter.21
  460.5 44.6 reduce-scatter.15
  508.9 33.8 reduce-scatter.17
  546.2 51.9 all-reduce.44
where the time goes:
time: 747 us; the launch traced here: 741 us
  waiting for transfers between devices  267 us (36%)
  matrix products  199 us (27%)
  blocking collectives  111 us (15%)
  local copies, waits for them, and re-layouts  85.3 us (11%)
  other arithmetic  45.7 us (6%)
  between operations  17.8 us (2%)
  starting transfers between devices  13 us (2%)
    psum x3, waiting for transfers between devices, head_total(): lax.psum(partial_sum.astype(jnp.bfloat16), 'head').astype(jnp.float32)  120 us
    unnamed x355, local copies, waits for them, and re-layouts  42.5 us
    psum x1, blocking collectives, per_device(): lax.psum((gain_in_part, gain_out_part, gain_ffn_part), ('seq', 'head'))  40.1 us
    psum x1, blocking collectives, per_device(): grad_conv_w, grad_decay = lax.psum((grad_conv_part, grad_decay_part), 'seq')  37 us
    all_gather x1, waiting for transfers between devices, per_device(): lax.all_gather(w_up.astype(jnp.bfloat16), 'seq', axis=0, tiled=True)  32.1 us
    dot_general x16, matrix products, advance(): jnp.einsum('bcd,bdw->bcw', weight, state, precision=HIGHEST_LEVEL)  24 us
    all_gather x1, waiting for transfers between devices, per_device(): lax.all_gather(w_out.astype(jnp.bfloat16), 'seq', axis=2, tiled=True)  23.6 us
    all_gather x1, waiting for transfers between devices, per_device(): lax.all_gather(w_down.astype(jnp.bfloat16), 'seq', axis=1, tiled=True)  23.5 us
  transfers between devices with their start and end apart: 18, of which 12 were waited for; matrix products, arithmetic and copies ran while one was open for 27% of the time, Pallas kernels for 0%

commit v1 on v0

v1 whole, which is shorter than its diff:
```python
import functools
import math

import jax
import jax.numpy as jnp
from jax import lax
from jax.experimental import pallas as pl
from jax.experimental.pallas import tpu as pltpu
from jax.sharding import PartitionSpec as P

D = 1024
KEY_SIZE = 128
VALUE_SIZE = 256
CONV = 4
BLOCK_TOKENS = 64
FG = 352
QKVG = 768
CONV_CH = 512


EPSILON = 1e-06
MOMENTUM = 0.95
RATE = 0.05
RATE_SMALL = 0.3
NEWTON_A = 3.4445
NEWTON_B = -4.775
NEWTON_C = 2.0315
NEWTON_STEPS = 5
HIGHEST_LEVEL = lax.Precision.HIGHEST


def shifted_2(block, axis, distance):
    devices = range(lax.axis_size(axis))
    route = [(i - distance, i) for i in devices if i - distance in devices]
    return lax.ppermute(block, axis, route)


def silu(value):
    return value * jax.nn.sigmoid(value)


def rms_unit(value_rows):
    return value_rows * lax.rsqrt(
        jnp.mean(value_rows * value_rows, axis=-1, keepdims=True) + EPSILON
    )


def rms_back(value_rows, gain, upstream):
    scale = lax.rsqrt(jnp.mean(value_rows * value_rows, axis=-1, keepdims=True) + EPSILON)
    unit = value_rows * scale
    inner = upstream * gain
    return scale * (inner - unit * jnp.mean(inner * unit, axis=-1, keepdims=True))


def keep_factors(document_start_mask):
    length = document_start_mask.shape[0]
    alive = 1.0 - document_start_mask
    padded = jnp.concatenate([jnp.ones((CONV - 1,), jnp.float32), alive])
    columns = [jnp.ones((length,), jnp.float32)]
    for tap in range(1, CONV):
        columns.append(columns[-1] * padded[CONV - tap : CONV - tap + length])
    return jnp.stack(columns, 1)


def tail_factors(alive):
    length = alive.shape[0]
    factors = [jnp.ones((), jnp.float32)]
    for back in range(1, CONV - 1):
        factors.insert(0, factors[0] * alive[length - back])
    return jnp.stack(factors)


def convolve(extended, conv_w, keep):
    length = keep.shape[0]
    total_sum = jnp.zeros((length,) + extended.shape[1:], jnp.float32)
    for tap in range(CONV):
        total_sum = (
            total_sum
            + conv_w[tap]
            * extended[CONV - 1 - tap : CONV - 1 - tap + length]
            * keep[:, tap, None]
        )
    return total_sum


def strengths(output_logits, decay):
    write_strength = jax.nn.sigmoid(output_logits[:, 1])
    gate_logarithm = -jnp.exp(decay[0]) * jax.nn.softplus(output_logits[:, 0] + decay[1])
    return (write_strength, gate_logarithm)


def dot_of(a, b, left, right):
    return lax.dot_general(
        a,
        b,
        (((left,), (right,)), ((), ())),
        precision=HIGHEST_LEVEL,
        preferred_element_type=jnp.float32,
    )


@jax.custom_vjp
def mm(a, b):
    return dot_of(a, b, 1, 0)


mm.defvjp(
    lambda a, b: (dot_of(a, b, 1, 0), (a, b)),
    lambda kept, g: (dot_of(g, kept[1], 1, 1), dot_of(kept[0], g, 0, 0)),
)


@jax.custom_vjp
def mm_nt(a, b):
    return dot_of(a, b, 1, 1)


mm_nt.defvjp(
    lambda a, b: (dot_of(a, b, 1, 1), (a, b)),
    lambda kept, g: (dot_of(g, kept[1], 1, 0), dot_of(g, kept[0], 0, 0)),
)


@jax.custom_vjp
def mm_tn(a, b):
    return dot_of(a, b, 0, 0)


mm_tn.defvjp(
    lambda a, b: (dot_of(a, b, 0, 0), (a, b)),
    lambda kept, g: (dot_of(kept[1], g, 1, 1), dot_of(kept[0], g, 1, 0)),
)


def cut_rows(array):
    return tuple(
        array[at : at + BLOCK_TOKENS] for at in range(0, array.shape[0], BLOCK_TOKENS)
    )


@jax.custom_vjp
def split_rows(array):
    return cut_rows(array)


split_rows.defvjp(
    lambda array: (cut_rows(array), None), lambda kept, g: (jnp.concatenate(g, 0),)
)


@jax.custom_vjp
def given_inverse(negated, inverse):
    return inverse


def given_inverse_back(inverse, g):
    return (dot_of(dot_of(inverse, g, 0, 0), inverse, 1, 1), jnp.zeros_like(g))


given_inverse.defvjp(lambda negated, inverse: (inverse, inverse), given_inverse_back)


def block_masks(span):
    length = span.shape[0]
    rows = lax.broadcasted_iota(jnp.int32, (length, length), 0)
    cols = lax.broadcasted_iota(jnp.int32, (length, length), 1)
    together = (rows // BLOCK_TOKENS) == (cols // BLOCK_TOKENS)
    lower = jnp.where(together & (rows >= cols), 1.0, 0.0)
    strict = jnp.where(together & (rows > cols), 1.0, 0.0)
    upper = jnp.where(together & (rows < cols), 1.0, 0.0)

    def count(matrix, marks):
        return jnp.dot(
            matrix.astype(jnp.bfloat16),
            marks.astype(jnp.bfloat16),
            preferred_element_type=jnp.float32,
        )

    wide = jnp.broadcast_to(span, (length, KEY_SIZE))
    same = jnp.where(count(lower, span * strict) < 0.5, lower, 0.0)
    head_mask = jnp.where(count(lower, wide) < 0.5, 1.0, 0.0)
    tail_mask = jnp.where(count(upper, wide) < 0.5, 1.0, 0.0)
    whole = jnp.broadcast_to(span, (length, VALUE_SIZE))
    last_masks = [
        jnp.where(jnp.sum(part, axis=0, keepdims=True) < 0.5, 1.0, 0.0) for part in cut_rows(whole)
    ]
    return (lower, strict, upper, same, head_mask, tail_mask, last_masks)


def prepare(masks, mixed_q, mixed_k, mixed_v, beta, glog, saved_inverse):
    lower, strict, upper, same, head_mask, tail_mask, last_masks = masks
    length = mixed_q.shape[0]
    active_q = silu(mixed_q)
    active_k = silu(mixed_k)
    values = silu(mixed_v)
    query = (
        active_q
        * lax.rsqrt(jnp.sum(active_q * active_q, axis=-1, keepdims=True) + EPSILON)
        * KEY_SIZE ** (-0.5)
    )
    keys = active_k * lax.rsqrt(jnp.sum(active_k * active_k, axis=-1, keepdims=True) + EPSILON)
    wide = jnp.broadcast_to(glog, (length, KEY_SIZE))
    whole = jnp.broadcast_to(glog, (length, VALUE_SIZE))
    decay_mat = jnp.exp(mm(lower, glog * strict)) * same
    head_part = jnp.exp(mm(lower, wide)) * head_mask
    tail_part = jnp.exp(mm(upper, wide)) * tail_mask
    lasts = [
        jnp.exp(jnp.sum(part, axis=0, keepdims=True)) * mask
        for part, mask in zip(split_rows(whole), last_masks)
    ]
    keys_beta = keys * beta
    negated = -mm_nt(keys_beta, keys) * decay_mat * strict
    if saved_inverse is None:
        rows = lax.broadcasted_iota(jnp.int32, (length, length), 0)
        cols = lax.broadcasted_iota(jnp.int32, (length, length), 1)
        identity = jnp.where(rows == cols, 1.0, 0.0)
        inverse = identity + negated
        power = negated
        for level in range(BLOCK_TOKENS.bit_length() - 2):
            power = mm(power, power)
            inverse = inverse + mm(inverse, power)
    else:
        inverse = given_inverse(negated, saved_inverse)
    weights = mm(inverse, keys_beta * head_part)
    targets = mm(inverse, values * beta)
    scores = mm_nt(query, keys) * decay_mat
    return (query * head_part, weights, targets, scores, keys * tail_part, lasts, inverse)


def run_core(masks, saved_inverse, mixed_q, mixed_k, mixed_v, beta, glog, state):
    queries, weights, targets, scores, keyed, lasts, unused = prepare(
        masks, mixed_q, mixed_k, mixed_v, beta, glog, saved_inverse
    )
    fresh_values = []
    results = []
    for query, weight, target, key, last in zip(
        split_rows(queries), split_rows(weights), split_rows(targets), split_rows(keyed), lasts
    ):
        fresh = target - mm(weight, state)
        results.append(mm(query, state))
        fresh_values.append(fresh)
        state = last * state + mm_tn(key, fresh)
    attended = jnp.concatenate(results, 0) + mm(scores, jnp.concatenate(fresh_values, 0))
    return (attended, state)


def forward_kernel(head_count, mixed_ref, beta_ref, glog_ref, span_ref, carried_ref, fresh_ref, pair_ref, inverse_ref):
    masks = block_masks(span_ref[...])
    rows = lax.broadcasted_iota(jnp.int32, (KEY_SIZE, KEY_SIZE), 0)
    cols = lax.broadcasted_iota(jnp.int32, (KEY_SIZE, KEY_SIZE), 1)
    for head in range(head_count):
        at = head * CONV_CH
        queries, weights, targets, scores, keyed, lasts, inverse = prepare(
            masks,
            mixed_ref[:, at : at + KEY_SIZE],
            mixed_ref[:, at + KEY_SIZE : at + 2 * KEY_SIZE],
            mixed_ref[:, at + 2 * KEY_SIZE : at + CONV_CH],
            beta_ref[head],
            glog_ref[head],
            None,
        )
        inverse_ref[head] = inverse
        transfer = jnp.where(rows == cols, 1.0, 0.0)
        offset = jnp.zeros((KEY_SIZE, VALUE_SIZE), jnp.float32)
        moved = []
        moved_query = []
        fresh_values = []
        results = []
        for query, weight, target, key, last in zip(
            cut_rows(queries), cut_rows(weights), cut_rows(targets), cut_rows(keyed), lasts
        ):
            lost = -dot_of(weight, transfer, 1, 0)
            fresh = target - dot_of(weight, offset, 1, 0)
            moved_query.append(dot_of(query, transfer, 1, 0))
            results.append(dot_of(query, offset, 1, 0))
            moved.append(lost)
            fresh_values.append(fresh)
            transfer = last[:, :KEY_SIZE] * transfer + dot_of(key, lost, 0, 0)
            offset = last * offset + dot_of(key, fresh, 0, 0)
        carried_ref[:, head * KEY_SIZE : (head + 1) * KEY_SIZE] = jnp.concatenate(
            moved_query, 0
        ) + dot_of(scores, jnp.concatenate(moved, 0), 1, 0)
        fresh_ref[:, head * VALUE_SIZE : (head + 1) * VALUE_SIZE] = jnp.concatenate(
            results, 0
        ) + dot_of(scores, jnp.concatenate(fresh_values, 0), 1, 0)
        pair_ref[head, :, :KEY_SIZE] = transfer.astype(jnp.bfloat16)
        pair_ref[head, :, KEY_SIZE:] = offset.astype(jnp.bfloat16)


def gated_norm(attended, gate_part, norm_out):
    return (
        attended
        * lax.rsqrt(jnp.mean(attended * attended, axis=-1, keepdims=True) + EPSILON)
        * norm_out
        * silu(gate_part)
    )


def carry_kernel(head_count, pair_ref, carried_ref, fresh_ref, gate_ref, norm_ref, attended_ref, gated_ref, state_ref):
    place = lax.axis_index("seq")
    for head in range(head_count):

        def step(at, state):
            return dot_of(
                pair_ref[at, head, :, :KEY_SIZE].astype(jnp.float32), state, 1, 0
            ) + pair_ref[at, head, :, KEY_SIZE:].astype(jnp.float32)

        state = lax.fori_loop(0, place, step, jnp.zeros((KEY_SIZE, VALUE_SIZE), jnp.float32))
        state_ref[head] = state
        part = slice(head * VALUE_SIZE, (head + 1) * VALUE_SIZE)
        attended = fresh_ref[:, part] + dot_of(
            carried_ref[:, head * KEY_SIZE : (head + 1) * KEY_SIZE], state, 1, 0
        )
        attended_ref[:, part] = attended
        gated_ref[:, part] = gated_norm(
            attended, gate_ref[:, part].astype(jnp.float32), norm_ref[...]
        ).astype(jnp.bfloat16)


def gate_back_kernel(head_count, upstream_ref, attended_ref, gate_ref, norm_ref, carried_ref, d_attended_ref, d_gate_ref, gain_ref, local_ref):
    gain_total = jnp.zeros((1, VALUE_SIZE), jnp.float32)
    norm_out = norm_ref[...]
    for head in range(head_count):
        part = slice(head * VALUE_SIZE, (head + 1) * VALUE_SIZE)
        attended = attended_ref[:, part]
        gate = gate_ref[:, part].astype(jnp.float32)
        upstream = upstream_ref[:, part]
        scale = lax.rsqrt(jnp.mean(attended * attended, axis=-1, keepdims=True) + EPSILON)
        unit = attended * scale
        sigma = jax.nn.sigmoid(gate)
        open_gate = gate * sigma
        gain_total = gain_total + jnp.sum(upstream * open_gate * unit, axis=0, keepdims=True)
        inner = upstream * open_gate * norm_out
        d_attended = scale * (inner - unit * jnp.mean(inner * unit, axis=-1, keepdims=True))
        d_gate = upstream * unit * norm_out * sigma * (1.0 + gate * (1.0 - sigma))
        d_attended_ref[:, part] = d_attended
        d_gate_ref[:, part] = d_gate.astype(jnp.bfloat16)
        local_ref[head] = dot_of(
            carried_ref[:, head * KEY_SIZE : (head + 1) * KEY_SIZE], d_attended, 0, 0
        ).astype(jnp.bfloat16)
    gain_ref[...] = gain_total


def back_kernel(head_count, pair_ref, local_ref, d_attended_ref, state_ref, inverse_ref, mixed_ref, beta_ref, glog_ref, span_ref, d_mixed_ref, d_beta_ref, d_glog_ref):
    count = lax.axis_size("seq")
    ahead = count - 1 - lax.axis_index("seq")
    masks = block_masks(span_ref[...])
    for head in range(head_count):

        def step(index, state):
            source = count - 1 - index
            return dot_of(
                pair_ref[source, head, :, :KEY_SIZE].astype(jnp.float32), state, 0, 0
            ) + local_ref[source, head].astype(jnp.float32)

        later = lax.fori_loop(0, ahead, step, jnp.zeros((KEY_SIZE, VALUE_SIZE), jnp.float32))
        at = head * CONV_CH
        unused, pull = jax.vjp(
            functools.partial(run_core, masks, inverse_ref[head]),
            mixed_ref[:, at : at + KEY_SIZE],
            mixed_ref[:, at + KEY_SIZE : at + 2 * KEY_SIZE],
            mixed_ref[:, at + 2 * KEY_SIZE : at + CONV_CH],
            beta_ref[head],
            glog_ref[head],
            state_ref[head],
        )
        d_q, d_k, d_v, d_beta, d_glog, unused_state = pull(
            (d_attended_ref[:, head * VALUE_SIZE : (head + 1) * VALUE_SIZE], later)
        )
        d_mixed_ref[:, at : at + KEY_SIZE] = d_q
        d_mixed_ref[:, at + KEY_SIZE : at + 2 * KEY_SIZE] = d_k
        d_mixed_ref[:, at + 2 * KEY_SIZE : at + CONV_CH] = d_v
        d_beta_ref[head] = d_beta
        d_glog_ref[head] = d_glog


def newton_kernel(batch_ref, out_ref):
    for index in range(batch_ref.shape[0]):
        wide = batch_ref[index].astype(jnp.float32)
        total_sum = jnp.sum(jnp.sum(wide * wide, axis=0, keepdims=True), axis=1, keepdims=True)
        current = (wide / (jnp.sqrt(total_sum) + 1e-07)).astype(jnp.bfloat16)
        for turn in range(NEWTON_STEPS):
            gram = lax.dot_general(
                current, current, (((0,), (0,)), ((), ())), preferred_element_type=jnp.float32
            ).astype(jnp.bfloat16)
            poly = (
                NEWTON_B * gram.astype(jnp.float32)
                + NEWTON_C * jnp.dot(gram, gram, preferred_element_type=jnp.float32)
            ).astype(jnp.bfloat16)
            current = (
                NEWTON_A * current.astype(jnp.float32)
                + jnp.dot(current, poly, preferred_element_type=jnp.float32)
            ).astype(jnp.bfloat16)
        out_ref[index] = current


def call_kernel(body, shapes, name, *operands):
    return pl.pallas_call(
        body,
        out_shape=[jax.ShapeDtypeStruct(shape, kind) for shape, kind in shapes],
        in_specs=[pl.BlockSpec(memory_space=pltpu.VMEM)] * len(operands),
        out_specs=[pl.BlockSpec(memory_space=pltpu.VMEM)] * len(shapes),
        compiler_params=pltpu.CompilerParams(vmem_limit_bytes=48 * 1024 * 1024),
        name=name,
    )(*operands)


def head_total(partial_sum):
    return lax.psum(partial_sum.astype(jnp.bfloat16), "head").astype(jnp.float32)


def per_device(
    tokens,
    doc_start,
    cotangent,
    norm_in,
    w_in,
    w_gates,
    conv_w,
    decay,
    norm_out,
    w_out,
    norm_ffn,
    w_up,
    w_down,
    moment_norm_in,
    moment_w_in,
    moment_w_gates,
    moment_conv_w,
    moment_decay,
    moment_norm_out,
    moment_w_out,
    moment_norm_ffn,
    moment_w_up,
    moment_w_down,
):
    length = tokens.shape[0]
    head_count = w_in.shape[1]
    hidden = w_up.shape[2]
    owners = lax.axis_size("seq")
    in_cols = head_count * QKVG
    gate_cols_count = 2 * head_count
    padding = -gate_cols_count % KEY_SIZE
    full_in = lax.all_gather(
        jnp.concatenate(
            [
                w_in.reshape(-1, in_cols),
                w_gates.reshape(-1, gate_cols_count),
                jnp.zeros((w_in.shape[0], padding), jnp.float32),
            ],
            1,
        ).astype(jnp.bfloat16),
        "seq",
        axis=0,
        tiled=True,
    )
    full_out = lax.all_gather(w_out.astype(jnp.bfloat16), "seq", axis=2, tiled=True)
    full_up = lax.all_gather(w_up.astype(jnp.bfloat16), "seq", axis=0, tiled=True)
    full_down = lax.all_gather(w_down.astype(jnp.bfloat16), "seq", axis=1, tiled=True)
    document_start_mask = doc_start.astype(jnp.float32)
    alive = 1.0 - document_start_mask
    span = document_start_mask[:, None]
    unit_in = rms_unit(tokens)
    normed_in = (unit_in * norm_in).astype(jnp.bfloat16)
    projected = jnp.dot(normed_in, full_in, preferred_element_type=jnp.float32)
    proj = lax.optimization_barrier(projected[:, :in_cols].astype(jnp.bfloat16))
    output_logits = projected[:, in_cols : in_cols + gate_cols_count].reshape(
        length, 2, head_count
    )
    conv_in = jnp.concatenate(
        [proj[:, head * QKVG : head * QKVG + CONV_CH] for head in range(head_count)], 1
    )
    gate_part = jnp.concatenate(
        [proj[:, head * QKVG + CONV_CH : (head + 1) * QKVG] for head in range(head_count)], 1
    )
    edge_scale = tail_factors(alive)
    edge = (conv_in[length - CONV + 1 :].astype(jnp.float32) * edge_scale[:, None]).astype(
        jnp.bfloat16
    )
    before = shifted_2(edge, "seq", 1)
    extended = jnp.concatenate([before, conv_in]).astype(jnp.float32)
    keep = keep_factors(document_start_mask)
    conv_flat = conv_w.reshape(CONV, -1)
    mixed, mixed_pull = jax.vjp(lambda e, w: convolve(e, w, keep), extended, conv_flat)
    (beta, glog), strength_pull = jax.vjp(strengths, output_logits, decay)
    beta_cols = beta.T[:, :, None]
    glog_cols = glog.T[:, :, None]
    wide_f32 = (length, head_count * VALUE_SIZE)
    square = (head_count, KEY_SIZE, VALUE_SIZE)
    carried, fresh, pair, inverse = call_kernel(
        functools.partial(forward_kernel, head_count),
        [
            ((length, head_count * KEY_SIZE), jnp.float32),
            (wide_f32, jnp.float32),
            ((head_count, KEY_SIZE, KEY_SIZE + VALUE_SIZE), jnp.bfloat16),
            ((head_count, length, length), jnp.float32),
        ],
        "delta_forward",
        mixed,
        beta_cols,
        glog_cols,
        span,
    )
    pairs = lax.all_gather(pair, "seq")
    attended, gated_b, incoming = call_kernel(
        functools.partial(carry_kernel, head_count),
        [(wide_f32, jnp.float32), (wide_f32, jnp.bfloat16), (square, jnp.float32)],
        "delta_carry",
        pairs,
        carried,
        fresh,
        gate_part,
        norm_out[None],
    )
    out_flat = full_out.reshape(head_count * VALUE_SIZE, -1)
    residual = tokens + head_total(
        jnp.dot(gated_b, out_flat, preferred_element_type=jnp.float32)
    )
    unit_ffn = rms_unit(residual)
    normed_ffn = (unit_ffn * norm_ffn).astype(jnp.bfloat16)
    ffn_pre = jnp.einsum("td,dgf->tgf", normed_ffn, full_up, preferred_element_type=jnp.float32)
    gate_pre = ffn_pre[:, 0]
    lift = ffn_pre[:, 1]
    active = (silu(gate_pre) * lift).astype(jnp.bfloat16)
    output = residual + head_total(jnp.dot(active, full_down, preferred_element_type=jnp.float32))
    cot_b = cotangent.astype(jnp.bfloat16)
    grad_down_part = jnp.einsum("tf,td->fd", active, cot_b, preferred_element_type=jnp.float32)
    d_active = jnp.einsum("td,fd->tf", cot_b, full_down, preferred_element_type=jnp.float32)
    sigma = jax.nn.sigmoid(gate_pre)
    d_gate_pre = d_active * lift * sigma * (1.0 + gate_pre * (1.0 - sigma))
    d_lift = d_active * gate_pre * sigma
    d_ffn_pre = jnp.stack([d_gate_pre, d_lift], 1).astype(jnp.bfloat16)
    grad_up_part = jnp.einsum(
        "td,tgf->dgf", normed_ffn, d_ffn_pre, preferred_element_type=jnp.float32
    )
    d_ffn_part = jnp.einsum("tgf,dgf->td", d_ffn_pre, full_up, preferred_element_type=jnp.float32)
    gain_ffn_part = jnp.sum(d_ffn_part * unit_ffn, 0)
    d_residual = cotangent + rms_back(residual, norm_ffn, head_total(d_ffn_part))
    res_b = d_residual.astype(jnp.bfloat16)
    grad_out_part = jnp.einsum("tv,td->vd", gated_b, res_b, preferred_element_type=jnp.float32)
    d_gated = jnp.einsum("td,vd->tv", res_b, out_flat, preferred_element_type=jnp.float32)
    d_attended, d_gate_part, gain_out_row, local_gradient = call_kernel(
        functools.partial(gate_back_kernel, head_count),
        [
            (wide_f32, jnp.float32),
            (wide_f32, jnp.bfloat16),
            ((1, VALUE_SIZE), jnp.float32),
            (square, jnp.bfloat16),
        ],
        "gate_back",
        d_gated,
        attended,
        gate_part,
        norm_out[None],
        carried,
    )
    gain_out_part = gain_out_row[0]
    local_gradients = lax.all_gather(local_gradient, "seq")
    d_mixed, d_beta, d_glog = call_kernel(
        functools.partial(back_kernel, head_count),
        [
            (mixed.shape, jnp.float32),
            (beta_cols.shape, jnp.float32),
            (beta_cols.shape, jnp.float32),
        ],
        "delta_back",
        pairs,
        local_gradients,
        d_attended,
        incoming,
        inverse,
        mixed,
        beta_cols,
        glog_cols,
        span,
    )
    d_extended, grad_conv_flat = mixed_pull(d_mixed)
    grad_conv_part = grad_conv_flat.reshape(conv_w.shape)
    d_logits, grad_decay_part = strength_pull((d_beta[:, :, 0].T, d_glog[:, :, 0].T))
    returned_edge = shifted_2(d_extended[: CONV - 1], "seq", -1)
    inner = d_extended[CONV - 1 :]
    d_conv_in = jnp.concatenate(
        [
            inner[: length - CONV + 1],
            inner[length - CONV + 1 :] + returned_edge * edge_scale[:, None],
        ]
    ).astype(jnp.bfloat16)
    columns = []
    for head in range(head_count):
        columns.append(d_conv_in[:, head * CONV_CH : (head + 1) * CONV_CH])
        columns.append(d_gate_part[:, head * VALUE_SIZE : (head + 1) * VALUE_SIZE])
    columns.append(d_logits.reshape(length, gate_cols_count).astype(jnp.bfloat16))
    columns.append(jnp.zeros((length, padding), jnp.bfloat16))
    d_proj = jnp.concatenate(columns, 1)
    grad_in_part = jnp.einsum("td,tc->dc", normed_in, d_proj, preferred_element_type=jnp.float32)
    d_in_part = jnp.einsum("tc,dc->td", d_proj, full_in, preferred_element_type=jnp.float32)
    gain_in_part = jnp.sum(d_in_part * unit_in, 0)
    grad_tokens = d_residual + rms_back(tokens, norm_in, head_total(d_in_part))
    grad_in_rows = lax.psum_scatter(
        grad_in_part.astype(jnp.bfloat16), "seq", scatter_dimension=0, tiled=True
    ).astype(jnp.float32)
    grad_w_in = grad_in_rows[:, :in_cols].reshape(w_in.shape)
    grad_w_gates = grad_in_rows[:, in_cols : in_cols + gate_cols_count].reshape(w_gates.shape)
    grad_w_out, grad_w_up, grad_w_down = (
        lax.psum_scatter(
            grad_out_part.reshape(head_count, VALUE_SIZE, -1).astype(jnp.bfloat16),
            "seq",
            scatter_dimension=2,
            tiled=True,
        ).astype(jnp.float32),
        lax.psum_scatter(
            grad_up_part.astype(jnp.bfloat16), "seq", scatter_dimension=0, tiled=True
        ).astype(jnp.float32),
        lax.psum_scatter(
            grad_down_part.astype(jnp.bfloat16), "seq", scatter_dimension=1, tiled=True
        ).astype(jnp.float32),
    )
    grad_conv_w, grad_decay = lax.psum((grad_conv_part, grad_decay_part), "seq")
    grad_norm_in, grad_norm_out, grad_norm_ffn = lax.psum(
        (gain_in_part, gain_out_part, gain_ffn_part), ("seq", "head")
    )
    small_scale = RATE_SMALL / math.sqrt(length * owners)

    def small_update(weight, moment, grad):
        fresh_moment = MOMENTUM * moment + grad
        return (weight - small_scale * (grad + MOMENTUM * fresh_moment), fresh_moment)

    new_norm_in, new_moment_norm_in = small_update(norm_in, moment_norm_in, grad_norm_in)
    new_w_gates, new_moment_w_gates = small_update(w_gates, moment_w_gates, grad_w_gates)
    new_conv_w, new_moment_conv_w = small_update(conv_w, moment_conv_w, grad_conv_w)
    new_decay, new_moment_decay = small_update(decay, moment_decay, grad_decay)
    new_norm_out, new_moment_norm_out = small_update(norm_out, moment_norm_out, grad_norm_out)
    new_norm_ffn, new_moment_norm_ffn = small_update(norm_ffn, moment_norm_ffn, grad_norm_ffn)
    new_moment_w_in = MOMENTUM * moment_w_in + grad_w_in
    look_in = grad_w_in + MOMENTUM * new_moment_w_in
    new_moment_w_out = MOMENTUM * moment_w_out + grad_w_out
    look_out = grad_w_out + MOMENTUM * new_moment_w_out
    new_moment_w_up = MOMENTUM * moment_w_up + grad_w_up
    look_up = grad_w_up + MOMENTUM * new_moment_w_up
    new_moment_w_down = MOMENTUM * moment_w_down + grad_w_down
    look_down = grad_w_down + MOMENTUM * new_moment_w_down
    bounds = ((0, KEY_SIZE), (KEY_SIZE, 2 * KEY_SIZE), (2 * KEY_SIZE, CONV_CH), (CONV_CH, QKVG))
    pieces = []
    widths = []
    for head in range(head_count):
        for lower_col, upper_col in bounds:
            pieces.append(look_in[:, head, lower_col:upper_col])
            widths.append(upper_col - lower_col)
        pieces.append(look_out[head].T)
        widths.append(VALUE_SIZE)
    groups = hidden // FG
    for group in range(groups):
        pieces.append(look_up[:, 0, group * FG : (group + 1) * FG])
        pieces.append(look_up[:, 1, group * FG : (group + 1) * FG])
        pieces.append(look_down[group * FG : (group + 1) * FG].T)
        widths.extend([FG, FG, FG])
    rounded_pieces = [piece.astype(jnp.bfloat16) for piece in pieces]
    count = len(rounded_pieces)
    rows = rounded_pieces[0].shape[0]
    widest = max(widths)
    per_owner = -(-count // owners)
    padded = [jnp.pad(piece, ((0, 0), (0, widest - piece.shape[1]))) for piece in rounded_pieces]
    padded = padded + [jnp.zeros((rows, widest), jnp.bfloat16)] * (owners * per_owner - count)
    outgoing = jnp.stack(padded).reshape(owners, per_owner, rows, widest)
    arrived = lax.all_to_all(outgoing, "seq", split_axis=0, concat_axis=2, tiled=True)[0]
    finished = call_kernel(newton_kernel, [(arrived.shape, jnp.bfloat16)], "newton", arrived)[0][
        None
    ]
    returned = lax.all_to_all(finished, "seq", split_axis=2, concat_axis=0, tiled=True)
    flat = returned.reshape(owners * per_owner, rows, widest)
    orthos = [flat[index, :, : widths[index]] for index in range(count)]
    updates = [
        orthos[index].astype(jnp.float32) * (RATE * 0.2 * math.sqrt(max(D, widths[index])))
        for index in range(count)
    ]
    cursor = 0
    in_heads = []
    out_heads = []
    for head in range(head_count):
        in_heads.append(jnp.concatenate(updates[cursor : cursor + 4], -1))
        out_heads.append(updates[cursor + 4].T)
        cursor += 5
    gate_cols = []
    lift_cols = []
    down_rows = []
    for group in range(groups):
        gate_cols.append(updates[cursor])
        lift_cols.append(updates[cursor + 1])
        down_rows.append(updates[cursor + 2].T)
        cursor += 3
    new_w_in = w_in - jnp.stack(in_heads, 1)
    new_w_out = w_out - jnp.stack(out_heads, 0)
    new_w_up = w_up - jnp.stack([jnp.concatenate(gate_cols, -1), jnp.concatenate(lift_cols, -1)], 1)
    new_w_down = w_down - jnp.concatenate(down_rows, 0)
    return (
        output,
        grad_tokens,
        grad_norm_in,
        grad_w_in,
        grad_w_gates,
        grad_conv_w,
        grad_decay,
        grad_norm_out,
        grad_w_out,
        grad_norm_ffn,
        grad_w_up,
        grad_w_down,
        new_norm_in,
        new_w_in,
        new_w_gates,
        new_conv_w,
        new_decay,
        new_norm_out,
        new_w_out,
        new_norm_ffn,
        new_w_up,
        new_w_down,
        new_moment_norm_in,
        new_moment_w_in,
        new_moment_w_gates,
        new_moment_conv_w,
        new_moment_decay,
        new_moment_norm_out,
        new_moment_w_out,
        new_moment_norm_ffn,
        new_moment_w_up,
        new_moment_w_down,
    )


def solution(mesh):
    return jax.shard_map(
        per_device,
        mesh=mesh,
        in_specs=(
            P("seq", None),
            P("seq"),
            P("seq", None),
            P(),
            P("seq", "head", None),
            P("seq", None, "head"),
            P(None, "head", None),
            P(None, "head"),
            P(),
            P("head", None, "seq"),
            P(),
            P("seq", None, "head"),
            P("head", "seq"),
            P(),
            P("seq", "head", None),
            P("seq", None, "head"),
            P(None, "head", None),
            P(None, "head"),
            P(),
            P("head", None, "seq"),
            P(),
            P("seq", None, "head"),
            P("head", "seq"),
        ),
        out_specs=(
            P("seq", None),
            P("seq", None),
            P(),
            P("seq", "head", None),
            P("seq", None, "head"),
            P(None, "head", None),
            P(None, "head"),
            P(),
            P("head", None, "seq"),
            P(),
            P("seq", None, "head"),
            P("head", "seq"),
            P(),
            P("seq", "head", None),
            P("seq", None, "head"),
            P(None, "head", None),
            P(None, "head"),
            P(),
            P("head", None, "seq"),
            P(),
            P("seq", None, "head"),
            P("head", "seq"),
            P(),
            P("seq", "head", None),
            P("seq", None, "head"),
            P(None, "head", None),
            P(None, "head"),
            P(),
            P("head", None, "seq"),
            P(),
            P("seq", None, "head"),
            P("head", "seq"),
        ),
        check_vma=False,
    )
```

time: 747 us -> 657 us (0.88)
  matrix products: 199 us -> 35.3 us
  waiting for transfers between devices: 267 us -> 351 us
  Pallas kernels: 0 us -> 58.5 us
  blocking collectives: 111 us -> 74.1 us
  local copies, waits for them, and re-layouts: 85.3 us -> 57.3 us
    dot_general x128 -> x6, matrix products: 180 us -> 16 us  [the longest x1 4.29 us: per_device(): jnp.einsum('tc,dc->td', d_proj, full_in, preferred_element_type=jnp.float32)]
    pallas_call x0 -> x5, Pallas kernels: none -> 58.5 us  [call_kernel(): pl.pallas_call(body, out_shape=[jax.ShapeDtypeStruct(shape, kind) for sha...]
    unnamed x19 -> x16, waiting for transfers between devices: 20.6 us -> 70.3 us
    reduce_scatter x0 -> x1, waiting for transfers between devices: none -> 48.1 us  [per_device(): lax.psum_scatter(grad_in_part.astype(jnp.bfloat16), 'seq', scatter_dimens...]
    psum x3, waiting for transfers between devices: 120 us -> 80.1 us  [head_total(): lax.psum(partial_sum.astype(jnp.bfloat16), 'head').astype(jnp.float32)]
    all_gather x3 -> x0, blocking collectives: 34.1 us -> none  [the longest x1 13 us: carried_in(): lax.all_gather(a.astype(kind), axis)]
    all_gather x3, waiting for transfers between devices: 31 us -> 59.8 us  [the longest x1 33.5 us: per_device(): lax.all_gather(jnp.concatenate([w_in.reshape(-1, in_cols), w_gates.reshap...]
    dynamic_update_slice x12 -> x0, local copies, waits for them, and re-layouts: 10.3 us -> none  [block_recurrence(): final_state, block_results = lax.scan(advance, initial_state, pieces)]
  transfers between devices with their start and end apart: 18 -> 17, of which waited for: 12 -> 12; matrix products, arithmetic and copies ran while one was open for 27% -> 13% of each run, Pallas kernels for 0% -> 4%
where the time goes in v1:
time: 657 us; the launch traced here: 645 us
  waiting for transfers between devices  351 us (53%)
  blocking collectives  74.1 us (11%)
  Pallas kernels  58.5 us (9%)
  local copies, waits for them, and re-layouts  57.3 us (9%)
  other arithmetic  39.2 us (6%)
  matrix products  35.3 us (5%)
  between operations  17 us (3%)
  starting transfers between devices  12.7 us (2%)
    psum x3, waiting for transfers between devices, head_total(): lax.psum(partial_sum.astype(jnp.bfloat16), 'head').astype(jnp.float32)  80.1 us
    unnamed x16, waiting for transfers between devices  70.3 us
    pallas_call x5, Pallas kernels, call_kernel(): pl.pallas_call(body, out_shape=[jax.ShapeDtypeStruct(shape, kind) for sha...  58.5 us
    reduce_scatter x1, waiting for transfers between devices, per_device(): lax.psum_scatter(grad_in_part.astype(jnp.bfloat16), 'seq', scatter_dimens...  48.1 us
    psum x1, blocking collectives, per_device(): lax.psum((gain_in_part, gain_out_part, gain_ffn_part), ('seq', 'head'))  40.3 us
    unnamed x231, local copies, waits for them, and re-layouts  39 us
    psum x1, blocking collectives, per_device(): grad_conv_w, grad_decay = lax.psum((grad_conv_part, grad_decay_part), 'seq')  33.8 us
    all_gather x1, waiting for transfers between devices, per_device(): lax.all_gather(jnp.concatenate([w_in.reshape(-1, in_cols), w_gates.reshap...  33.5 us
  transfers between devices with their start and end apart: 17, of which 12 were waited for; matrix products, arithmetic and copies ran while one was open for 13% of the time, Pallas kernels for 4%

profile of v1, /device:TPU:0, one launch (start us, length us, event | category | flops | bytes accessed | tf_op | source)
XLA Modules:
  0.0 645.1 jit_solution(1899694540155433282)
XLA Ops:
  13.1 33.5 %all-gather.9.cloned.1.call-done = bf16[1024,1664]{1,0:T(8,128)(2,1)} async-done(((bf16[128,1664]{1,0:T(8,128)(2,1)}), bf16[1024,1664]{1,0:T(8,128)(2,1)}) %all-gather.9.cloned.1.call-update) | async-done | bytes 3407888 | tf_op jit(solution)/shard_map/all_gather | solution.py:444
  55.9 15.9 %delta_forward.1 = (f32[256,256]{1,0:T(8,128)S(1)}, f32[256,512]{1,0:T(8,128)S(1)}, bf16[2,128,384]{2,1,0:T(8,128)(2,1)}, f32[2,256,256]{2,1,0:T(8,128)S(1)}) custom-call(f32[256,1024]{1,0:T(8,128)S(1)} %multiply_add_fusion.2.mixed_ref, f32[2,256,1]{2,1,0:T(8,128)S(1)} %copy.126.beta_ref, f32[2,256,1]{2,1,0:T(8,128)S(1)} %copy.127.glog_ref, ...), custom_call_target="tpu_custom_call" | custom-call | tf_op jit(solution)/shard_map/delta_forward/pallas_call | solution.py:398
  74.5 26.4 %all-gather.17.cloned.1.call-done = bf16[16,128,384]{2,1,0:T(8,128)(2,1)} async-done(((bf16[2,128,384]{2,1,0:T(8,128)(2,1)}), bf16[16,128,384]{2,1,0:T(8,128)(2,1)}) %all-gather.17.cloned.1.call-update) | async-done | bytes 1572880 | tf_op jit(solution)/shard_map/all_gather | solution.py:504
  103.9 22.9 %all-gather.11.cloned.1.call-done = bf16[2,256,1024]{2,1,0:T(8,128)(2,1)} async-done(((bf16[2,256,128]{2,1,0:T(8,128)(2,1)}), bf16[2,256,1024]{2,1,0:T(8,128)(2,1)}) %all-gather.11.cloned.1.call-update) | async-done | bytes 1048592 | tf_op jit(solution)/shard_map/all_gather | solution.py:457
  132.1 36.1 %all-reduce.30.cloned.1.call-done = bf16[256,1024]{1,0:T(8,128)(2,1)} async-done(((bf16[256,1024]{1,0:T(8,128)(2,1)}), bf16[256,1024]{1,0:T(8,128)(2,1)}) %all-reduce.30.cloned.1.call-update) | async-done | bytes 524304 | tf_op jit(solution)/shard_map/psum | solution.py:409
  170.7 31.2 %all-gather.13.cloned.1.call-done = bf16[1024,2,704]{0,2,1:T(8,128)(2,1)} async-done(((bf16[128,2,704]{0,2,1:T(8,128)(2,1)}), bf16[1024,2,704]{0,2,1:T(8,128)(2,1)}) %all-gather.13.cloned.1.call-update) | async-done | bytes 2883600 | tf_op jit(solution)/shard_map/all_gather | solution.py:458
  202.0 4.3 fusion.18
  206.2 23.3 %all-gather.15.cloned.1.call-done = bf16[704,1024]{1,0:T(8,128)(2,1)} async-done(((bf16[704,128]{1,0:T(8,128)(2,1)}), bf16[704,1024]{1,0:T(8,128)(2,1)}) %all-gather.15.cloned.1.call-update) | async-done | bytes 1441808 | tf_op jit(solution)/shard_map/all_gather | solution.py:459
  229.5 3.7 fusion.2
  235.5 38.7 %all-reduce.32.cloned.1.call-done = bf16[256,1024]{1,0:T(8,128)(2,1)} async-done(((bf16[256,1024]{1,0:T(8,128)(2,1)}), bf16[256,1024]{1,0:T(8,128)(2,1)}) %all-reduce.32.cloned.1.call-update) | async-done | bytes 524304 | tf_op jit(solution)/shard_map/psum | solution.py:409
  299.3 4.6 copy.149
  306.9 27.6 %delta_back.1 = (f32[256,1024]{1,0:T(8,128)S(1)}, f32[2,256,1]{2,1,0:T(8,128)S(1)}, f32[2,256,1]{2,1,0:T(8,128)S(1)}) custom-call(bf16[8,2,128,384]{3,2,1,0:T(8,128)(2,1)} %bitcast.261, bf16[8,2,128,256]{3,2,1,0:T(8,128)(2,1)S(1)} %bitcast.263, f32[256,512]{1,0:T(8,128)S(1)} %get-tuple-element.52.d_attended_ref, f32[2,128,256]{2,1,0:T(8,128)S(1)} %copy-done.5, ...), custom_call_target="tpu_custom_call" | custom-call | tf_op jit(solution)/shard_map/delta_back/pallas_call | solution.py:398
  356.7 28.9 %reduce-scatter.17.cloned.1.call-done = bf16[128,704]{1,0:T(8,128)(2,1)} async-done(((bf16[1024,704]{1,0:T(8,128)(2,1)}), bf16[128,704]{1,0:T(8,128)(2,1)}) %reduce-scatter.17.cloned.1.call-update) | async-done | bytes 180240
  388.2 4.3 fusion.43
  392.6 41.2 %reduce-scatter.15.cloned.1.call-done = bf16[128,1408]{1,0:T(8,128)(2,1)} async-done(((bf16[1024,1408]{1,0:T(8,128)(2,1)}), bf16[128,1408]{1,0:T(8,128)(2,1)}) %reduce-scatter.15.cloned.1.call-update) | async-done | bytes 360464
  436.4 48.1 %reduce-scatter.11.cloned.1.call-done = bf16[128,1664]{1,0:T(8,128)(2,1)} async-done(((bf16[1024,1664]{1,0:T(8,128)(2,1)}), bf16[128,1664]{1,0:T(8,128)(2,1)}) %reduce-scatter.11.cloned.1.call-update) | async-done | bytes 426000 | tf_op jit(solution)/shard_map/reduce_scatter | solution.py:599
  489.9 3.7 all-to-all-start
  497.6 33.8 %all-reduce.24 = (f32[4,2,512]{2,1,0:T(2,128)}, f32[2,2]{1,0:T(2,128)}) all-reduce(f32[4,2,512]{2,1,0:T(2,128)} %reshape.292, f32[2,2]{1,0:T(2,128)} %pad_add_fusion.3), channel_id=1, replica_groups=mesh['seq'=8,'head'=4] {'seq'}, use_global_device_ids=true, to_apply=%region_15.16 | all-reduce | flops 4100 | bytes 32800 | tf_op jit(solution)/shard_map/psum | solution.py:618
  534.1 5.3 all-reduce.34.cloned.1.call-done
  541.5 40.3 %all-reduce.23 = (f32[1024]{0:T(1024)S(1)}, f32[256]{0:T(256)S(1)}, f32[1024]{0:T(1024)S(1)}) all-reduce(f32[1024]{0:T(1024)} %get-tuple-element.226, f32[256]{0:T(256)S(1)} %bitcast.266, f32[1024]{0:T(1024)} %get-tuple-element.224), channel_id=1, replica_groups=mesh['seq'=8,'head'=4] {'seq','head'}, use_global_device_ids=true, to_apply=%region_9.10 | all-reduce | flops 2304 | bytes 18432 | tf_op jit(solution)/shard_map/psum | solution.py:619
  587.5 13.2 %newton.1 = bf16[2,1024,352]{2,1,0:T(8,128)(2,1)S(1)} custom-call(bf16[2,1024,352]{2,1,0:T(8,128)(2,1)S(1)} %bitcast.259), custom_call_target="tpu_custom_call" | custom-call | tf_op jit(solution)/shard_map/newton/pallas_call | solution.py:398
  603.5 4.4 all-to-all-start.1
  613.7 15.3 %all-to-all-done.1 = bf16[1,2,1024,352]{3,1,0,2:T(2,128)(2,1)} async-done(((bf16[1,2,1024,352]{3,1,0,2:T(2,128)(2,1)}), bf16[1,2,1024,352]{3,1,0,2:T(2,128)(2,1)}, u32[]{:S(2)}, u32[]{:S(2)}) %all-to-all-start.1) | async-done | bytes 1441824 | tf_op jit(solution)/shard_map/all_to_all | solution.py:669
  629.0 3.7 copy.139
  (364 shorter events, 117.7 us)
Async XLA Ops:
  7.2 39.3 %all-gather.9.cloned.1.call-start = ((), (), s32[]{:S(2)}) async-start(), calls=%async_computation.6 | async-start | bytes 3833856 | tf_op jit(solution)/shard_map/all_gather | solution.py:444
  9.8 91.0 %all-gather.17.cloned.1.call-start = ((), (), s32[]{:S(2)}) async-start(), calls=%async_computation.13 | async-start | bytes 1769472 | tf_op jit(solution)/shard_map/all_gather | solution.py:504
  9.9 44.3 %copy-start.60 = (f32[1,4,2,128]{3,1,2,0:T(4,128)}, f32[1,4,2,128]{3,1,2,0:T(4,128)S(1)}, u32[]{:S(2)}) copy-start(f32[1,4,2,128]{3,1,2,0:T(4,128)S(1)} %copy.155) | copy-start | bytes 12292
  9.9 44.3 %copy-start.62 = (f32[1,4,2,128]{3,1,2,0:T(4,128)}, f32[1,4,2,128]{3,1,2,0:T(4,128)S(1)}, u32[]{:S(2)}) copy-start(f32[1,4,2,128]{3,1,2,0:T(4,128)S(1)} %copy.154) | copy-start | bytes 12292
  10.0 44.3 %copy-start.64 = (f32[1,4,2,128]{3,1,2,0:T(4,128)}, f32[1,4,2,128]{3,1,2,0:T(4,128)S(1)}, u32[]{:S(2)}) copy-start(f32[1,4,2,128]{3,1,2,0:T(4,128)S(1)} %copy.153) | copy-start | bytes 12292
  50.8 3.3 collective-permute-start
  55.9 44.9 %copy-start.9 = (f32[256]{0:T(256)S(1)}, f32[256]{0:T(256)}, u32[]{:S(2)}) copy-start(f32[256]{0:T(256)} %param.31) | copy-start | bytes 3076
  72.6 54.2 %all-gather.11.cloned.1.call-start = ((), (), s32[]{:S(2)}) async-start(), calls=%async_computation.7 | async-start | bytes 1179648 | tf_op jit(solution)/shard_map/all_gather | solution.py:457
  73.4 94.8 %all-reduce.30.cloned.1.call-start = ((), (), s32[]{:S(2)}) async-start(), calls=%async_computation.8 | async-start | bytes 1048576 | tf_op jit(solution)/shard_map/psum | solution.py:409
  129.3 72.7 %all-gather.13.cloned.1.call-start = ((), (), s32[]{:S(2)}) async-start(), calls=%async_computation.9 | async-start | bytes 3244032 | tf_op jit(solution)/shard_map/all_gather | solution.py:458
  131.3 98.2 %all-gather.15.cloned.1.call-start = ((), (), s32[]{:S(2)}) async-start(), calls=%async_computation.10 | async-start | bytes 1622016 | tf_op jit(solution)/shard_map/all_gather | solution.py:459
  132.1 69.9 %copy-start.56 = (f32[1024]{0:T(1024)S(1)}, f32[1024]{0:T(1024)}, u32[]{:S(2)}) copy-start(f32[1024]{0:T(1024)} %param.33) | copy-start | bytes 12292
  132.1 142.1 %all-reduce.32.cloned.1.call-start = ((), (), s32[]{:S(2)}) async-start(), calls=%async_computation.11 | async-start | bytes 1048576 | tf_op jit(solution)/shard_map/psum | solution.py:409
  170.7 106.3 %copy-start.71 = (f32[256]{0:T(256)}, f32[256]{0:T(256)S(1)}, u32[]{:S(2)}) copy-start(f32[256]{0:T(256)S(1)} %add_rsqrt_fusion) | copy-start | bytes 3076
  235.4 70.2 %all-gather.19.cloned.1.call-start = ((), (), s32[]{:S(2)}) async-start(), calls=%async_computation.14 | async-start | bytes 1179648 | tf_op jit(solution)/shard_map/all_gather | solution.py:558
  281.5 73.2 %reduce-scatter.13.cloned.1.call-start = ((), (), s32[]{:S(2)}) async-start(), calls=%async_computation.15 | async-start | bytes 1179648
  288.0 97.6 %reduce-scatter.17.cloned.1.call-start = ((), (), s32[]{:S(2)}) async-start(), calls=%async_computation.17 | async-start | bytes 1769472
  294.5 139.3 %reduce-scatter.15.cloned.1.call-start = ((), (), s32[]{:S(2)}) async-start(), calls=%async_computation.16 | async-start | bytes 3244032
  304.0 180.5 %reduce-scatter.11.cloned.1.call-start = ((), (), s32[]{:S(2)}) async-start(), calls=%async_computation.12 | async-start | bytes 3833856 | tf_op jit(solution)/shard_map/reduce_scatter | solution.py:599
  337.3 5.7 collective-permute-start.1
  348.3 191.1 %all-reduce.34.cloned.1.call-start = ((), (), s32[]{:S(2)}) async-start(), calls=%async_computation.18 | async-start | bytes 2097152 | tf_op jit(solution)/shard_map/psum | solution.py:409
  489.9 49.5 %copy-start.45 = (f32[256,1024]{1,0:T(8,128)S(1)}, f32[256,1024]{1,0:T(8,128)}, u32[]{:S(2)}) copy-start(f32[256,1024]{1,0:T(8,128)} %get-tuple-element.319) | copy-start | bytes 3145732
  489.9 94.4 %all-to-all-start = ((bf16[8,2,128,352]{2,3,1,0:T(8,128)(2,1)}), bf16[8,2,128,352]{2,3,1,0:T(8,128)(2,1)S(1)}, u32[]{:S(2)}, u32[]{:S(2)}) async-start(bf16[8,2,128,352]{2,3,1,0:T(8,128)(2,1)} %bitcast.278), calls=%async_computation.1 | async-start | bytes 2883584 | tf_op jit(solution)/shard_map/all_to_all | solution.py:665
  603.5 25.4 %all-to-all-start.1 = ((bf16[1,2,1024,352]{3,1,0,2:T(2,128)(2,1)}), bf16[1,2,1024,352]{3,1,0,2:T(2,128)(2,1)}, u32[]{:S(2)}, u32[]{:S(2)}) async-start(bf16[1,2,1024,352]{3,1,0,2:T(2,128)(2,1)} %copy.138), calls=%async_computation.2 | async-start | bytes 3145728 | tf_op jit(solution)/shard_map/all_to_all | solution.py:669
  (92 other events, 924.3 us)
Sparse Core Ops, SparseCore 0:
  10.5 35.9 all-gather.8
  72.8 28.0 all-gather.16
  103.3 23.4 all-gather.10
  129.6 38.6 all-reduce.29
  170.5 31.3 all-gather.12
  204.3 25.1 all-gather.14
  235.5 38.6 all-reduce.31
  281.6 23.1 all-gather.18
  308.0 36.0 reduce-scatter.12
  347.2 38.3 reduce-scatter.16
  389.0 44.7 reduce-scatter.14
  437.1 47.3 reduce-scatter.10
  487.4 51.9 all-reduce.33
